TPU v7x, 32 devices: a whole 2x2x4 slice. The times are simulated.
32 devices in a mesh: group: 1, req: 4 (over z), head: 4 (over y, x), pool: 2 (over core).
Axes of the slice: x: 2, y: 2, z: 4, core: 2. Of those that a mesh axis runs over, the one named last changes fastest.
Arguments:
- queries: bfloat16 [192, 4096], P(('group', 'req'), 'head'), may hold values from -128 to 128
- new_entries: bfloat16 [192, 2, 4, 256], P(('group', 'req'), None, 'head'), may hold values from -6 to 6
- cache_pages: bfloat16 [4, 416, 16, 256], P('head', ('group', 'req', 'pool')), may hold values from -6 to 6
- page_table: int32 [192, 2, 1], P(('group', 'req'), 'pool'), may hold values from 0 to 51, as said below
- cached_length: int32 [192, 2], P(('group', 'req'), 'pool'), may hold values from 1 to 16, as said below
- leave_slots: int32 [32], P(('group', 'req', 'pool')), may hold values from 0 to 50, as said below
- arrive_slots: int32 [32], P(('group', 'req', 'pool')), may hold values from 0 to 51, as said below
- residual: bfloat16 [192, 2048], P(('group', 'req', 'head')), may hold values from -5 to 5
- norm_gain: float32 [2048], replicated, may hold values from 0.5 to 1.5
- output_weight: bfloat16 [4096, 2048], P(('head', 'pool')), may hold values from -0.25 to 0.25
- expert_choice: int32 [192, 8], P(('group', 'req', 'head')), may hold values from 0 to 15, all different within a row; in each aligned block of 12 rows (0 to 11, 12 to 23, ...) at most 12 rows name the same one
- route_weight: float32 [192, 8], P(('group', 'req', 'head')), may hold values from 0.2 to 1
- gate_up: bfloat16 [16, 2, 384, 2048], P(('req', 'head'), None, 'pool'), may hold values from -0.125 to 0.125
- down_weight: bfloat16 [16, 384, 2048], P(('req', 'head'), 'pool'), may hold values from -0.3125 to 0.3125
Outputs:
- decoded: bfloat16 [192, 2048], P(('group', 'req', 'head'), 'pool')
Inputs may be any that keep to these rules, and one draw needn't show every extreme that they name: `page_table`: within each block of one index of req and one pool, the 48 entries name distinct slots, none of them among that block's leave_slots. `leave_slots`: each block's 4 entries are distinct. `arrive_slots`: each block's 4 entries are distinct slots that its page table names. `cached_length`: in every block of 48 requests and each pool some request has 16. `expert_choice`: each row names 8 distinct experts; in each aligned block of 12 rows no expert is named more than 12 times, a bound that some block reaches.
All inputs are finite; a program needn't handle non-finite values.
Results may differ from a plain program's by a relative error of at most 0.023.
Values may be sent and summed in bfloat16 or wider, within the bound.
A program may use at most 64 MiB of HBM per device.

v0:
```python
import jax
import jax.numpy as jnp
from jax import lax
from jax.sharding import PartitionSpec as P


def swapped(value, axis, apart):
    mask = 2**apart
    pairs = [(source, source ^ mask) for source in range(lax.axis_size(axis))]
    return lax.ppermute(value, axis, pairs)


def combined_all(shard, axis, join):
    gathered = jax.tree.map(
        lambda a, kind: lax.all_gather(a.astype(kind), axis),
        shard,
        (jnp.bfloat16, jnp.bfloat16, jnp.bfloat16),
    )

    def take(source):
        return jax.tree.map(
            lambda a, own: lax.dynamic_index_in_dim(a, source, 0, False).astype(own.dtype),
            gathered,
            shard,
        )

    return lax.fori_loop(
        1, lax.axis_size(axis), lambda source, state: join(state, take(source)), take(0)
    )


def merge_parts(earlier, later):
    first_max, first_denominator, first_value = earlier
    second_max, second_denominator, second_value = later
    largest = jnp.maximum(first_max, second_max)
    first_scale = jnp.exp(first_max - largest)
    second_scale = jnp.exp(second_max - largest)
    denominator = first_denominator * first_scale + second_denominator * second_scale
    weighted = first_value * first_scale[..., None] + second_value * second_scale[..., None]
    return (largest, denominator, weighted)


def local(
    queries,
    new_entries,
    cache_pages,
    page_table,
    cached_length,
    leave_slots,
    arrive_slots,
    residual,
    norm_gain,
    output_weight,
    expert_choice,
    route_weight,
    gate_up,
    down_weight,
):
    batch_size = queries.shape[0]
    group_count = cache_pages.shape[0]
    head_dim = new_entries.shape[3] // 2
    group_size = queries.shape[1] // (group_count * head_dim)
    pool_index = lax.axis_index("pool")
    outgoing = cache_pages[:, leave_slots]
    arrived = swapped(outgoing, "pool", 0)
    current = cache_pages.at[:, arrive_slots].set(arrived)
    context = current[:, page_table[:, 0, :]]
    context = context.reshape(group_count, batch_size, -1, 2 * head_dim)
    context_keys = context[..., :head_dim]
    context_values = context[..., head_dim:]
    grouped_queries = queries.reshape(batch_size, group_count, group_size, head_dim)
    score_scale = head_dim ** (-0.5)
    attention_scores = (
        jnp.einsum(
            "bgqd,gbtd->bgqt", grouped_queries, context_keys, preferred_element_type=jnp.float32
        )
        * score_scale
    )
    positions = jnp.arange(context.shape[2], dtype=jnp.int32)
    valid_mask = positions[None, :] < cached_length
    attention_scores = jnp.where(valid_mask[:, None, None, :], attention_scores, -jnp.inf)
    fresh_scores = (
        jnp.einsum(
            "bgqd,bsgd->bgqs",
            grouped_queries,
            new_entries[..., :head_dim],
            preferred_element_type=jnp.float32,
        )
        * score_scale
    )
    fresh_scores = jnp.where(pool_index == 0, fresh_scores, -jnp.inf)
    largest = jnp.maximum(jnp.max(attention_scores, axis=-1), jnp.max(fresh_scores, axis=-1))
    local_weights = jnp.exp(attention_scores - largest[..., None])
    fresh_weights = jnp.exp(fresh_scores - largest[..., None])
    denominator = jnp.sum(local_weights, axis=-1) + jnp.sum(fresh_weights, axis=-1)
    weighted = jnp.einsum("bgqt,gbtd->bgqd", local_weights, context_values.astype(jnp.float32))
    weighted = weighted + jnp.einsum(
        "bgqs,bsgd->bgqd", fresh_weights, new_entries[..., head_dim:].astype(jnp.float32)
    )
    largest, denominator, weighted = combined_all(
        (largest, denominator, weighted), "pool", merge_parts
    )
    attended = (weighted / denominator[..., None]).reshape(batch_size, -1).astype(jnp.bfloat16)
    head_width = output_weight.shape[0]
    own_heads = lax.dynamic_slice_in_dim(attended, pool_index * head_width, head_width, 1)
    partial_value = jnp.dot(own_heads, output_weight, preferred_element_type=jnp.float32)
    rows_here = residual.shape[0]
    summed = lax.psum(partial_value.astype(jnp.bfloat16), ("head", "pool")).astype(jnp.float32)
    attention = lax.dynamic_slice_in_dim(summed, lax.axis_index("head") * rows_here, rows_here, 0)
    hidden = residual.astype(jnp.float32) + attention
    normed = (
        hidden * lax.rsqrt(jnp.mean(hidden * hidden, axis=-1, keepdims=True) + 1e-06) * norm_gain
    ).astype(jnp.bfloat16)
    expert_count = lax.axis_size("req") * lax.axis_size("head")
    top_count = expert_choice.shape[1]
    capacity = max(
        2, min(rows_here, (2 * rows_here * top_count + expert_count - 1) // expert_count)
    )
    flat_choice = expert_choice.reshape(-1)
    expert_hits = (
        flat_choice[:, None] == jnp.arange(expert_count, dtype=jnp.int32)[None, :]
    ).astype(jnp.int32)
    earlier = jnp.cumsum(expert_hits, axis=0) - expert_hits
    slot_index = jnp.sum(earlier * expert_hits, axis=1)
    target = flat_choice * capacity + slot_index
    placed = (
        target[:, None] == jnp.arange(expert_count * capacity, dtype=jnp.int32)[None, :]
    ).astype(jnp.float32)
    placed = placed.reshape(rows_here, top_count, expert_count * capacity)
    dispatch = jnp.sum(placed, axis=1).astype(jnp.bfloat16)
    combine_matrix = jnp.sum(placed * route_weight[:, :, None], axis=1)
    outgoing_rows = jnp.einsum("re,rd->ed", dispatch, normed, preferred_element_type=jnp.float32)
    outgoing_rows = outgoing_rows.astype(jnp.bfloat16).reshape(expert_count, capacity, -1)
    model_width = normed.shape[1]
    half_width = model_width // lax.axis_size("pool")
    projection = gate_up[0].reshape(-1, model_width)
    hidden_size = projection.shape[0] // 2
    received = lax.all_to_all(
        outgoing_rows, ("req", "head"), split_axis=0, concat_axis=0, tiled=True
    )
    sources = received.shape[0]
    item_count = received.shape[1]
    flat_rows = received.reshape(sources * item_count, model_width)
    projected = jnp.einsum("nd,fd->nf", flat_rows, projection, preferred_element_type=jnp.float32)
    activated = (jax.nn.silu(projected[:, :hidden_size]) * projected[:, hidden_size:]).astype(
        jnp.bfloat16
    )
    part_sum = jnp.dot(activated, down_weight[0], preferred_element_type=jnp.float32).reshape(
        sources, item_count, model_width
    )
    column_sum = lax.psum_scatter(
        part_sum.astype(jnp.bfloat16), "pool", scatter_dimension=2, tiled=True
    )
    returned = lax.all_to_all(column_sum, ("req", "head"), split_axis=0, concat_axis=0, tiled=True)
    gathered = returned.reshape(expert_count * capacity, half_width).astype(jnp.float32)
    expert_mix = jnp.dot(combine_matrix, gathered, precision=lax.Precision.HIGHEST)
    own_columns = lax.dynamic_slice_in_dim(hidden, pool_index * half_width, half_width, 1)
    return (own_columns + expert_mix).astype(jnp.bfloat16)


def solution(mesh):
    return jax.shard_map(
        local,
        mesh=mesh,
        in_specs=(
            P(("group", "req"), "head"),
            P(("group", "req"), None, "head", None),
            P("head", ("group", "req", "pool"), None, None),
            P(("group", "req"), "pool", None),
            P(("group", "req"), "pool"),
            P(("group", "req", "pool")),
            P(("group", "req", "pool")),
            P(("group", "req", "head"), None),
            P(),
            P(("head", "pool"), None),
            P(("group", "req", "head"), None),
            P(("group", "req", "head"), None),
            P(("req", "head"), None, "pool", None),
            P(("req", "head"), "pool", None),
        ),
        out_specs=P(("group", "req", "head"), "pool"),
        check_vma=False,
    )
```

profile of v0, /device:TPU:0, one launch (start us, length us, event | category | flops | bytes accessed | tf_op | source)
XLA Modules:
  0.0 159.7 jit_solution(2999815218880634779)
XLA Ops:
  6.5 0.0 copy-start
  6.5 0.0 copy-start.2
  6.5 0.0 copy-start.4
  6.5 0.0 all-reduce.2.cloned.1.call-start
  6.5 1.2 copy.73
  7.7 0.7 compare_select_fusion.1
  8.4 0.5 gather_fusion
  8.9 0.6 collective-permute-start
  9.5 0.7 fusion.23
  10.2 0.7 compare_select_fusion.2
  10.8 0.7 iota_compare_fusion.2
  11.5 0.8 copy.59
  12.3 0.1 eq.33
  12.4 0.1 fusion.12
  12.5 0.1 reduce_window_sum.11
  12.6 0.2 select_reduce_fusion.1
  12.8 0.1 reduce_sum.59
  12.9 0.9 copy.64
  13.8 1.0 fusion.25
  14.8 0.0 copy-done.4
  14.8 0.1 copy.61
  14.9 0.0 collective-permute-done
  14.9 0.6 scatter_fusion
  15.5 0.6 gather_fusion.1
  16.1 0.3 fusion.24
  16.4 0.1 fusion.14
  16.5 0.0 copy-done.2
  16.6 0.2 fusion.15
  16.8 0.1 copy.54
  16.9 1.8 %all-gather.3 = bf16[2,48,8]{1,2,0:T(8,128)(2,1)S(1)} all-gather(bf16[1,48,8]{1,2,0:T(8,128)(2,1)S(1)} %copy.54), channel_id=3, replica_groups=mesh['group'=1,'req'=4,'head'=4,'pool'=2] {'pool'}, dimensions={0}, use_global_device_ids=true | all-gather | bytes 2304 | tf_op jit(solution)/shard_map/all_gather | solution.py:15
  18.7 0.2 fusion.7
  18.9 0.1 copy.57
  19.0 1.8 %all-gather.4 = bf16[2,48,8]{1,2,0:T(8,128)(2,1)S(1)} all-gather(bf16[1,48,8]{1,2,0:T(8,128)(2,1)S(1)} %copy.57), channel_id=4, replica_groups=mesh['group'=1,'req'=4,'head'=4,'pool'=2] {'pool'}, dimensions={0}, use_global_device_ids=true | all-gather | bytes 2304 | tf_op jit(solution)/shard_map/all_gather | solution.py:15
  20.9 0.1 copy.55
  21.0 0.1 copy.58
  21.0 0.1 copy.56
  21.1 0.3 fusion.2
  21.4 1.9 %all-gather = bf16[96,8,128]{2,1,0:T(8,128)(2,1)S(1)} all-gather(bf16[48,8,128]{2,1,0:T(8,128)(2,1)S(1)} %fusion.2), channel_id=2, replica_groups=mesh['group'=1,'req'=4,'head'=4,'pool'=2] {'pool'}, dimensions={0}, use_global_device_ids=true | all-gather | bytes 294912 | tf_op jit(solution)/shard_map/all_gather | solution.py:15
  23.3 0.0 copy-start.1
  23.3 0.2 divide_convert_fusion
  23.6 0.0 copy-start.3
  23.6 0.0 copy-done
  23.6 1.2 convolution_convert_fusion.2
  24.8 0.0 all-reduce.2.cloned.1.call-update
  24.8 0.0 reduce-scatter.2.cloned.1.call-start
  24.8 0.1 convert_reduce_fusion
  25.0 56.1 %all-reduce.2.cloned.1.call-done = bf16[48,2048]{1,0:T(8,128)(2,1)} async-done(((bf16[48,2048]{1,0:T(8,128)(2,1)}), bf16[48,2048]{1,0:T(8,128)(2,1)}) %all-reduce.2.cloned.1.call-update) | async-done | bytes 196624 | tf_op jit(solution)/shard_map/psum | solution.py:108
  81.0 0.0 copy-done.1
  81.0 1.0 multiply_reduce_fusion
  82.1 0.0 copy-done.3
  82.1 1.3 convolution_convert_fusion.1
  83.4 1.3 reshape.273
  84.6 30.5 %all_to_all.10 = bf16[16,12,2048]{2,1,0:T(8,128)(2,1)} all-to-all(bf16[16,12,2048]{2,1,0:T(8,128)(2,1)S(1)} %reshape.273), channel_id=1, replica_groups=mesh['group'=1,'req'=4,'head'=4,'pool'=2] {'req','head'}, dimensions={0} | all-to-all | bytes 1572864 | tf_op jit(solution)/shard_map/all_to_all | solution.py:138
  115.1 1.3 reshape.274
  116.4 2.1 %fusion.26 = f32[192,384]{1,0:T(8,128)S(1)} fusion(bf16[192,2048]{1,0:T(8,128)(2,1)S(1)} %reshape.274, bf16[384,2048]{1,0:T(8,128)(2,1)} %bitcast.85), kind=kOutput, calls=%fused_computation.71 | convolution fusion | flops 301989888 | bytes 2654208 | tf_op jit(solution)/shard_map/nd,fd->nf/dot_general | solution.py:144
  118.5 0.1 fusion.6
  118.7 2.4 %convolution_convert_fusion = bf16[16,12,2048]{2,0,1:T(8,128)(2,1)} fusion(bf16[1,192,2048]{2,1,0:T(8,128)(2,1)} %param.27, bf16[16,12,192]{2,1,0:T(8,128)(2,1)S(1)} %dot_general.36), kind=kOutput, calls=%fused_computation.3 | convolution fusion | flops 151388160 | bytes 1646592 | tf_op jit(solution)/shard_map/dot_general | solution.py:148
  121.0 0.0 reduce-scatter.2.cloned.1.call-update
  121.1 6.6 %reduce-scatter.2.cloned.1.call-done = bf16[16,12,1024]{2,0,1:T(8,128)(2,1)} async-done(((bf16[16,12,2048]{2,0,1:T(8,128)(2,1)}), bf16[16,12,1024]{2,0,1:T(8,128)(2,1)}) %reduce-scatter.2.cloned.1.call-update) | async-done | bytes 393232 | tf_op jit(solution)/shard_map/reduce_scatter | solution.py:151
  127.6 2.0 %copy.63 = bf16[16,12,1024]{2,1,0:T(8,128)(2,1)} copy(bf16[16,12,1024]{2,0,1:T(8,128)(2,1)} %reduce-scatter.2.cloned.1.call-done) | data formatting | bytes 786432 | tf_op jit(solution)/shard_map/reduce_scatter | solution.py:151
  129.6 6.7 %all-to-all-start.1 = ((bf16[16,12,1024]{2,1,0:T(8,128)(2,1)}), bf16[16,12,1024]{2,1,0:T(8,128)(2,1)S(1)}, u32[]{:S(2)}, u32[]{:S(2)}) async-start(bf16[16,12,1024]{2,1,0:T(8,128)(2,1)} %copy.63), calls=%async_computation.2 | async-start | bytes 1048576 | tf_op jit(solution)/shard_map/all_to_all | solution.py:154
  136.4 15.5 %all-to-all-done.1 = bf16[16,12,1024]{2,1,0:T(8,128)(2,1)S(1)} async-done(((bf16[16,12,1024]{2,1,0:T(8,128)(2,1)}), bf16[16,12,1024]{2,1,0:T(8,128)(2,1)S(1)}, u32[]{:S(2)}, u32[]{:S(2)}) %all-to-all-start.1) | async-done | bytes 393248 | tf_op jit(solution)/shard_map/all_to_all | solution.py:154
  151.9 0.1 reshape.275
  151.9 0.9 fusion.4
  (9 shorter events, 0.1 us)
Async XLA Ops:
  6.5 17.1 %copy-start = (bf16[512,2048]{1,0:T(8,128)(2,1)S(1)}, bf16[512,2048]{1,0:T(8,128)(2,1)}, u32[]{:S(2)}) copy-start(bf16[512,2048]{1,0:T(8,128)(2,1)} %param.23) | copy-start | bytes 6291460
  6.5 10.0 %copy-start.2 = (bf16[48,2,1,256]{3,1,2,0:T(2,128)(2,1)S(1)}, bf16[48,2,1,256]{3,1,2,0:T(2,128)(2,1)}, u32[]{:S(2)}) copy-start(bf16[48,2,1,256]{3,1,2,0:T(2,128)(2,1)} %param.15) | copy-start | bytes 147460
  6.5 8.3 %copy-start.4 = (f32[12,8]{0,1:T(8,128)S(1)}, f32[12,8]{0,1:T(8,128)}, u32[]{:S(2)}) copy-start(f32[12,8]{0,1:T(8,128)} %param.25) | copy-start | bytes 1156
  6.5 74.5 %all-reduce.2.cloned.1.call-start = ((), (), s32[]{:S(2)}) async-start(), calls=%async_computation.3 | async-start | bytes 393216 | tf_op jit(solution)/shard_map/psum | solution.py:108
  8.9 6.0 %collective-permute-start = (bf16[1,4,16,256]{3,2,1,0:T(8,128)(2,1)S(1)}, bf16[1,4,16,256]{3,2,1,0:T(8,128)(2,1)S(1)}, u32[]{:S(2)}, u32[]{:S(2)}) collective-permute-start(bf16[1,4,16,256]{3,2,1,0:T(8,128)(2,1)S(1)} %bitcast.94), channel_id=1, source_target_pairs={{0,1},{1,0},{2,3},{3,2},{4,5},{5,4},{6,7},{7,6},{8,9},{9,8},{10,11... | collective-permute-start | bytes 98312 | tf_op jit(solution)/shard_map/ppermute | solution.py:10
  23.3 57.7 %copy-start.1 = (bf16[12,2048]{1,0:T(8,128)(2,1)S(1)}, bf16[12,2048]{1,0:T(8,128)(2,1)}, u32[]{:S(2)}) copy-start(bf16[12,2048]{1,0:T(8,128)(2,1)} %param.21) | copy-start | bytes 147460
  23.6 58.5 %copy-start.3 = (f32[2048]{0:T(1024)S(1)}, f32[2048]{0:T(1024)}, u32[]{:S(2)}) copy-start(f32[2048]{0:T(1024)} %param.22) | copy-start | bytes 24580
  24.8 102.8 %reduce-scatter.2.cloned.1.call-start = ((), (), s32[]{:S(2)}) async-start(), calls=%async_computation.4 | async-start | bytes 1179648 | tf_op jit(solution)/shard_map/reduce_scatter | solution.py:151
  129.6 22.2 %all-to-all-start.1 = ((bf16[16,12,1024]{2,1,0:T(8,128)(2,1)}), bf16[16,12,1024]{2,1,0:T(8,128)(2,1)S(1)}, u32[]{:S(2)}, u32[]{:S(2)}) async-start(bf16[16,12,1024]{2,1,0:T(8,128)(2,1)} %copy.63), calls=%async_computation.2 | async-start | bytes 1048576 | tf_op jit(solution)/shard_map/all_to_all | solution.py:154
Sparse Core Ops, SparseCore 0:
  24.9 56.0 all-reduce.1
  121.2 6.3 reduce-scatter.1
where the time goes:
time: 160 us
  waiting for transfers between devices  78.1 us (49%)
  blocking collectives  36.1 us (23%)
  between operations  13.6 us (8%)
  local copies, waits for them, and re-layouts  10 us (6%)
  matrix products  9.56 us (6%)
  starting transfers between devices  7.33 us (5%)
  other arithmetic  4.95 us (3%)
    psum x1, waiting for transfers between devices, local(): lax.psum(partial_value.astype(jnp.bfloat16), ('head', 'pool'))  56.1 us
    all_to_all x1, blocking collectives, local(): lax.all_to_all(outgoing_rows, ('req', 'head'), split_axis=0, concat_axis=...  30.5 us
    all_to_all x1, waiting for transfers between devices, local(): lax.all_to_all(column_sum, ('req', 'head'), split_axis=0, concat_axis=0,...  15.5 us
    all_to_all x1, starting transfers between devices, local(): lax.all_to_all(column_sum, ('req', 'head'), split_axis=0, concat_axis=0,...  6.73 us
    reduce_scatter x1, waiting for transfers between devices, local(): lax.psum_scatter(part_sum.astype(jnp.bfloat16), 'pool', scatter_dimension...  6.55 us
    all_gather x3, blocking collectives, combined_all(): lax.all_gather(a.astype(kind), axis)  5.63 us
  transfers between devices with their start and end apart: 4, of which 3 were waited for; matrix products, arithmetic and copies ran while one was open for 3% of the time, Pallas kernels for 0%

commit v1 on v0

--- a/solution.py
+++ b/solution.py
@@ -105,7 +105,9 @@
     own_heads = lax.dynamic_slice_in_dim(attended, pool_index * head_width, head_width, 1)
     partial_value = jnp.dot(own_heads, output_weight, preferred_element_type=jnp.float32)
     rows_here = residual.shape[0]
-    summed = lax.psum(partial_value.astype(jnp.bfloat16), ("head", "pool")).astype(jnp.float32)
+    summed = jnp.sum(
+        lax.all_gather(partial_value.astype(jnp.bfloat16), ("head", "pool")), axis=0
+    ).astype(jnp.float32)
     attention = lax.dynamic_slice_in_dim(summed, lax.axis_index("head") * rows_here, rows_here, 0)
     hidden = residual.astype(jnp.float32) + attention
     normed = (

time: 160 us -> 133 us (0.83)
  waiting for transfers between devices: 78.1 us -> 49.3 us
  blocking collectives: 36.1 us -> 37.9 us
    psum x1 -> x0, waiting for transfers between devices: 56.1 us -> none  [local(): lax.psum(partial_value.astype(jnp.bfloat16), ('head', 'pool'))]
    all_gather x0 -> x1, waiting for transfers between devices: none -> 27.1 us  [local(): lax.all_gather(partial_value.astype(jnp.bfloat16), ('head', 'pool'))]
    all_to_all x1, blocking collectives: 30.5 us -> 32.2 us  [local(): lax.all_to_all(outgoing_rows, ('req', 'head'), split_axis=0, concat_axis=...]
    reduce_sum x0 -> x1, other arithmetic: none -> 1.65 us  [local(): jnp.sum(lax.all_gather(partial_value.astype(jnp.bfloat16), ('head', 'pool...]
  transfers between devices with their start and end apart: 4 -> 4, of which waited for: 3 -> 3; matrix products, arithmetic and copies ran while one was open for 3% -> 4% of each run, Pallas kernels for 0% -> 0%
where the time goes in v1:
time: 133 us
  waiting for transfers between devices  49.3 us (37%)
  blocking collectives  37.9 us (28%)
  between operations  13.7 us (10%)
  matrix products  9.56 us (7%)
  local copies, waits for them, and re-layouts  9.3 us (7%)
  starting transfers between devices  7.34 us (6%)
  other arithmetic  5.73 us (4%)
    all_to_all x1, blocking collectives, local(): lax.all_to_all(outgoing_rows, ('req', 'head'), split_axis=0, concat_axis=...  32.2 us
    all_gather x1, waiting for transfers between devices, local(): lax.all_gather(partial_value.astype(jnp.bfloat16), ('head', 'pool'))  27.1 us
    all_to_all x1, waiting for transfers between devices, local(): lax.all_to_all(column_sum, ('req', 'head'), split_axis=0, concat_axis=0,...  15.5 us
    all_to_all x1, starting transfers between devices, local(): lax.all_to_all(column_sum, ('req', 'head'), split_axis=0, concat_axis=0,...  6.74 us
    reduce_scatter x1, waiting for transfers between devices, local(): lax.psum_scatter(part_sum.astype(jnp.bfloat16), 'pool', scatter_dimension...  6.64 us
    all_gather x3, blocking collectives, combined_all(): lax.all_gather(a.astype(kind), axis)  5.63 us
  transfers between devices with their start and end apart: 4, of which 3 were waited for; matrix products, arithmetic and copies ran while one was open for 4% of the time, Pallas kernels for 0%

profile of v1, /device:TPU:0, one launch (start us, length us, event | category | flops | bytes accessed | tf_op | source)
XLA Modules:
  0.0 132.8 jit_solution(10844197944778628042)
XLA Ops:
  6.5 0.0 copy-start
  6.5 0.0 copy-start.2
  6.5 0.0 all-gather.8.cloned.1.call-start
  6.5 1.2 copy.72
  7.7 0.7 compare_select_fusion.1
  8.4 0.5 gather_fusion
  8.9 0.6 collective-permute-start
  9.5 0.7 fusion.23
  10.2 0.7 compare_select_fusion.2
  10.8 0.7 iota_compare_fusion.2
  11.5 0.9 copy.64
  12.5 1.0 fusion.25
  13.4 0.0 collective-permute-done
  13.4 0.6 scatter_fusion
  14.1 0.6 gather_fusion.1
  14.7 0.3 fusion.24
  15.0 0.1 fusion.14
  15.1 0.0 copy-done.2
  15.1 0.2 fusion.15
  15.3 0.1 copy.54
  15.4 1.8 %all-gather.4 = bf16[2,48,8]{1,2,0:T(8,128)(2,1)S(1)} all-gather(bf16[1,48,8]{1,2,0:T(8,128)(2,1)S(1)} %copy.54), channel_id=3, replica_groups=mesh['group'=1,'req'=4,'head'=4,'pool'=2] {'pool'}, dimensions={0}, use_global_device_ids=true | all-gather | bytes 2304 | tf_op jit(solution)/shard_map/all_gather | solution.py:15
  17.3 0.2 fusion.7
  17.5 0.1 copy.57
  17.6 1.8 %all-gather.5 = bf16[2,48,8]{1,2,0:T(8,128)(2,1)S(1)} all-gather(bf16[1,48,8]{1,2,0:T(8,128)(2,1)S(1)} %copy.57), channel_id=4, replica_groups=mesh['group'=1,'req'=4,'head'=4,'pool'=2] {'pool'}, dimensions={0}, use_global_device_ids=true | all-gather | bytes 2304 | tf_op jit(solution)/shard_map/all_gather | solution.py:15
  19.4 0.1 copy.55
  19.5 0.1 copy.58
  19.6 0.1 copy.56
  19.6 0.3 fusion.2
  19.9 1.9 %all-gather = bf16[96,8,128]{2,1,0:T(8,128)(2,1)S(1)} all-gather(bf16[48,8,128]{2,1,0:T(8,128)(2,1)S(1)} %fusion.2), channel_id=2, replica_groups=mesh['group'=1,'req'=4,'head'=4,'pool'=2] {'pool'}, dimensions={0}, use_global_device_ids=true | all-gather | bytes 294912 | tf_op jit(solution)/shard_map/all_gather | solution.py:15
  21.9 0.0 copy-start.4
  21.9 0.2 divide_convert_fusion
  22.1 0.0 copy-done
  22.1 1.2 convolution_convert_fusion.2
  23.3 0.0 all-gather.8.cloned.1.call-update
  23.3 0.0 reduce-scatter.2.cloned.1.call-start
  23.4 0.0 copy-done.4
  23.4 0.1 copy.59
  23.5 0.1 eq.33
  23.5 0.0 copy-done.5
  23.6 0.1 copy.61
  23.6 0.1 fusion.12
  23.7 0.1 reduce_window_sum.11
  23.9 0.2 select_reduce_fusion.1
  24.0 0.1 reduce_sum.72
  24.1 0.1 convert_reduce_fusion
  24.3 27.1 %all-gather.8.cloned.1.call-done = bf16[384,2048]{1,0:T(8,128)(2,1)} async-done(((bf16[48,2048]{1,0:T(8,128)(2,1)}), bf16[384,2048]{1,0:T(8,128)(2,1)}) %all-gather.8.cloned.1.call-update) | async-done | bytes 1572880 | tf_op jit(solution)/shard_map/all_gather | solution.py:109
  51.4 1.7 %reduce_sum.70 = bf16[48,2048]{1,0:T(8,128)(2,1)S(1)} reduce(bf16[8,48,2048]{2,1,0:T(8,128)(2,1)} %bitcast.86, bf16[]{:T(256)} %constant.64.clone.1), dimensions={0}, to_apply=%region_5.6 | reduce | flops 688128 | bytes 1769474 | tf_op jit(solution)/shard_map/reduce_sum | solution.py:108
  53.1 0.0 copy-done.1
  53.1 0.2 multiply_reduce_fusion
  53.3 0.0 copy-done.3
  53.3 1.3 convolution_convert_fusion.1
  54.6 1.3 reshape.273
  55.8 32.2 %all_to_all.10 = bf16[16,12,2048]{2,1,0:T(8,128)(2,1)} all-to-all(bf16[16,12,2048]{2,1,0:T(8,128)(2,1)S(1)} %reshape.273), channel_id=1, replica_groups=mesh['group'=1,'req'=4,'head'=4,'pool'=2] {'req','head'}, dimensions={0} | all-to-all | bytes 1572864 | tf_op jit(solution)/shard_map/all_to_all | solution.py:140
  88.1 1.3 reshape.274
  89.4 2.1 %fusion.26 = f32[192,384]{1,0:T(8,128)S(1)} fusion(bf16[192,2048]{1,0:T(8,128)(2,1)S(1)} %reshape.274, bf16[384,2048]{1,0:T(8,128)(2,1)} %bitcast.87), kind=kOutput, calls=%fused_computation.71 | convolution fusion | flops 301989888 | bytes 2654208 | tf_op jit(solution)/shard_map/nd,fd->nf/dot_general | solution.py:146
  91.5 0.1 fusion.6
  91.6 2.4 %convolution_convert_fusion = bf16[16,12,2048]{2,0,1:T(8,128)(2,1)} fusion(bf16[1,192,2048]{2,1,0:T(8,128)(2,1)} %param.27, bf16[16,12,192]{2,1,0:T(8,128)(2,1)S(1)} %dot_general.36), kind=kOutput, calls=%fused_computation.3 | convolution fusion | flops 151388160 | bytes 1646592 | tf_op jit(solution)/shard_map/dot_general | solution.py:150
  94.0 0.0 reduce-scatter.2.cloned.1.call-update
  94.0 6.6 %reduce-scatter.2.cloned.1.call-done = bf16[16,12,1024]{2,0,1:T(8,128)(2,1)} async-done(((bf16[16,12,2048]{2,0,1:T(8,128)(2,1)}), bf16[16,12,1024]{2,0,1:T(8,128)(2,1)}) %reduce-scatter.2.cloned.1.call-update) | async-done | bytes 393232 | tf_op jit(solution)/shard_map/reduce_scatter | solution.py:153
  100.7 2.0 %copy.63 = bf16[16,12,1024]{2,1,0:T(8,128)(2,1)} copy(bf16[16,12,1024]{2,0,1:T(8,128)(2,1)} %reduce-scatter.2.cloned.1.call-done) | data formatting | bytes 786432 | tf_op jit(solution)/shard_map/reduce_scatter | solution.py:153
  102.7 6.7 %all-to-all-start.1 = ((bf16[16,12,1024]{2,1,0:T(8,128)(2,1)}), bf16[16,12,1024]{2,1,0:T(8,128)(2,1)S(1)}, u32[]{:S(2)}, u32[]{:S(2)}) async-start(bf16[16,12,1024]{2,1,0:T(8,128)(2,1)} %copy.63), calls=%async_computation.2 | async-start | bytes 1048576 | tf_op jit(solution)/shard_map/all_to_all | solution.py:156
  109.4 15.5 %all-to-all-done.1 = bf16[16,12,1024]{2,1,0:T(8,128)(2,1)S(1)} async-done(((bf16[16,12,1024]{2,1,0:T(8,128)(2,1)}), bf16[16,12,1024]{2,1,0:T(8,128)(2,1)S(1)}, u32[]{:S(2)}, u32[]{:S(2)}) %all-to-all-start.1) | async-done | bytes 393248 | tf_op jit(solution)/shard_map/all_to_all | solution.py:156
  124.9 0.1 reshape.275
  125.0 0.9 fusion.4
  (12 shorter events, 0.1 us)
Async XLA Ops:
  6.5 15.6 %copy-start = (bf16[512,2048]{1,0:T(8,128)(2,1)S(1)}, bf16[512,2048]{1,0:T(8,128)(2,1)}, u32[]{:S(2)}) copy-start(bf16[512,2048]{1,0:T(8,128)(2,1)} %param.23) | copy-start | bytes 6291460
  6.5 8.5 %copy-start.2 = (bf16[48,2,1,256]{3,1,2,0:T(2,128)(2,1)S(1)}, bf16[48,2,1,256]{3,1,2,0:T(2,128)(2,1)}, u32[]{:S(2)}) copy-start(bf16[48,2,1,256]{3,1,2,0:T(2,128)(2,1)} %param.15) | copy-start | bytes 147460
  6.5 44.9 %all-gather.8.cloned.1.call-start = ((), (), s32[]{:S(2)}) async-start(), calls=%async_computation.4 | async-start | bytes 1769472 | tf_op jit(solution)/shard_map/all_gather | solution.py:109
  8.9 4.5 %collective-permute-start = (bf16[1,4,16,256]{3,2,1,0:T(8,128)(2,1)S(1)}, bf16[1,4,16,256]{3,2,1,0:T(8,128)(2,1)S(1)}, u32[]{:S(2)}, u32[]{:S(2)}) collective-permute-start(bf16[1,4,16,256]{3,2,1,0:T(8,128)(2,1)S(1)} %bitcast.96), channel_id=1, source_target_pairs={{0,1},{1,0},{2,3},{3,2},{4,5},{5,4},{6,7},{7,6},{8,9},{9,8},{10,11... | collective-permute-start | bytes 98312 | tf_op jit(solution)/shard_map/ppermute | solution.py:10
  21.9 1.5 %copy-start.4 = (s32[12,8]{0,1:T(8,128)S(1)}, s32[12,8]{0,1:T(8,128)}, u32[]{:S(2)}) copy-start(s32[12,8]{0,1:T(8,128)} %param.24) | copy-start | bytes 1156
  21.9 1.7 %copy-start.5 = (f32[12,8]{0,1:T(8,128)S(1)}, f32[12,8]{0,1:T(8,128)}, u32[]{:S(2)}) copy-start(f32[12,8]{0,1:T(8,128)} %param.25) | copy-start | bytes 1156
  23.3 29.8 %copy-start.1 = (bf16[12,2048]{1,0:T(8,128)(2,1)S(1)}, bf16[12,2048]{1,0:T(8,128)(2,1)}, u32[]{:S(2)}) copy-start(bf16[12,2048]{1,0:T(8,128)(2,1)} %param.21) | copy-start | bytes 147460
  23.3 30.0 %copy-start.3 = (f32[2048]{0:T(1024)S(1)}, f32[2048]{0:T(1024)}, u32[]{:S(2)}) copy-start(f32[2048]{0:T(1024)} %param.22) | copy-start | bytes 24580
  23.3 77.4 %reduce-scatter.2.cloned.1.call-start = ((), (), s32[]{:S(2)}) async-start(), calls=%async_computation.3 | async-start | bytes 1179648 | tf_op jit(solution)/shard_map/reduce_scatter | solution.py:153
  102.7 22.2 %all-to-all-start.1 = ((bf16[16,12,1024]{2,1,0:T(8,128)(2,1)}), bf16[16,12,1024]{2,1,0:T(8,128)(2,1)S(1)}, u32[]{:S(2)}, u32[]{:S(2)}) async-start(bf16[16,12,1024]{2,1,0:T(8,128)(2,1)} %copy.63), calls=%async_computation.2 | async-start | bytes 1048576 | tf_op jit(solution)/shard_map/all_to_all | solution.py:156
Sparse Core Ops, SparseCore 0:
  23.4 27.9 all-gather.7
  94.2 6.4 reduce-scatter.1
